TPU v7x, 32 devices: a whole 2x2x4 slice. The times are simulated.
32 devices in a mesh: dp: 2 (over x), ctx: 4 (over y, core), tp: 4 (over z).
Axes of the slice: x: 2, y: 2, z: 4, core: 2. Of those that a mesh axis runs over, the one named last changes fastest.
Arguments:
- tokens: bfloat16 [16384, 768], P(('dp', 'ctx', 'tp')), may hold values from -6 to 6
- first_gain: bfloat16 [768], replicated, may hold values from 0.5 to 1.5
- first_bias: bfloat16 [768], replicated, may hold values from -0.4375 to 0.4375
- mixer_weight: bfloat16 [768, 3, 768], P(None, None, 'tp'), may hold values from -0.21875 to 0.21875
- mixer_bias: bfloat16 [3, 768], P(None, 'tp'), may hold values from -0.3125 to 0.3125
- feature_weight: bfloat16 [2, 12, 64, 64], P(None, 'tp'), may hold values from -1.5 to 1.5
- feature_bias: bfloat16 [2, 12, 64], P(None, 'tp'), may hold values from -6 to 6
- output_weight: bfloat16 [768, 768], P('tp'), may hold values from -6 to 6
- output_bias: bfloat16 [768], replicated, may hold values from -4 to 4
- second_gain: bfloat16 [768], replicated, may hold values from 0.5 to 1.5
- second_bias: bfloat16 [768], replicated, may hold values from -4 to 4
- inner_weight: bfloat16 [768, 3072], P(None, 'tp'), may hold values from -0.21875 to 0.21875
- inner_bias: bfloat16 [3072], P('tp'), may hold values from -4 to 4
- outer_weight: bfloat16 [3072, 768], P('tp'), may hold values from -0.109375 to 0.109375
- outer_bias: bfloat16 [768], replicated, may hold values from -4 to 4
- block_owner: int32 [2, 32], P('dp'), may hold values from 0 to 0, as said below
- cotangent: bfloat16 [16384, 768], P(('dp', 'ctx', 'tp')), may hold values from -6 to 6
Outputs:
- result: bfloat16 [16384, 768], P(('dp', 'ctx', 'tp'))
- tokens_gradient: float32 [16384, 768], P(('dp', 'ctx', 'tp'))
- first_gain_gradient: float32 [768], replicated
- first_bias_gradient: float32 [768], replicated
- mixer_weight_gradient: float32 [768, 3, 768], P(None, None, 'tp')
- mixer_bias_gradient: float32 [3, 768], P(None, 'tp')
- feature_weight_gradient: float32 [2, 12, 64, 64], P(None, 'tp')
- feature_bias_gradient: float32 [2, 12, 64], P(None, 'tp')
- output_weight_gradient: float32 [768, 768], P('tp')
- output_bias_gradient: float32 [768], replicated
- second_gain_gradient: float32 [768], replicated
- second_bias_gradient: float32 [768], replicated
- inner_weight_gradient: float32 [768, 3072], P(None, 'tp')
- inner_bias_gradient: float32 [3072], P('tp')
- outer_weight_gradient: float32 [3072, 768], P('tp')
- outer_bias_gradient: float32 [768], replicated
Inputs may be any that keep to these rules, and one draw needn't show every extreme that they name: `block_owner`: all blocks of one sequence carry one number, and pieces of a data group share the same blocks. A sequence covers 8192 // 256 or twice that many consecutive blocks of every piece, so it has 8192 or 16384 tokens; its number is the index of its last 8192-token unit, so numbers rise along a row, differ between sequences, and the last block of every row carries 1 - 1.
All inputs are finite; a program needn't handle non-finite values.
Results may differ from a plain program's by a relative error of at most 0.015.
Values may be sent and summed in bfloat16 or wider, within the bound.
A program may use at most 128 MiB of HBM per device.

v0:
```python
import jax
import jax.numpy as jnp
from jax import lax
from jax.sharding import PartitionSpec as P

HD = 64
BLOCK = 64
SHORT = 8192
EPSILON = 1e-05
HIGHEST = lax.Precision.HIGHEST


def entering(x, axis, combine, identity, reverse):
    peers, mine = (lax.axis_size(axis), lax.axis_index(axis))
    everything = jax.tree.map(lambda part: lax.all_gather(part, axis), x)
    start = jax.tree.map(
        lambda part, zero: jnp.broadcast_to(jnp.asarray(zero, part.dtype), part.shape), x, identity
    )

    def turn(k, before):
        at = peers - 1 - k if reverse else k
        reached = at > mine if reverse else at < mine
        new = combine(before, jax.tree.map(lambda part: part[at], everything))
        return jax.tree.map(lambda a, b: jnp.where(reached, a, b), new, before)

    return lax.fori_loop(0, peers, turn, start)


def layer_norm(values, norm_gain, norm_offset):
    average = jnp.mean(values, axis=-1, keepdims=True)
    centered = values - average
    variance = jnp.mean(centered * centered, axis=-1, keepdims=True)
    return centered * lax.rsqrt(variance + EPSILON) * norm_gain + norm_offset


def gaussian_unit(values):
    return (
        0.5
        * values
        * (1.0 + jnp.tanh(0.7978845608028654 * (values + 0.044715 * values * values * values)))
    )


def feature_map(inputs, weight, offset):
    logits = jnp.einsum("thd,hde->the", inputs, weight, precision=HIGHEST) + offset
    return jnp.concatenate(
        [jax.nn.softmax(logits, axis=-1), jax.nn.softmax(-logits, axis=-1)], axis=-1
    )


def rounded(values):
    return lax.optimization_barrier(values.astype(jnp.bfloat16)).astype(jnp.float32)


def add_pair(first_pair, second_pair):
    return (first_pair[0] + second_pair[0], first_pair[1] + second_pair[1])


def shards(
    tokens,
    first_gain,
    first_bias,
    mixer_weight,
    mixer_bias,
    feature_weight,
    feature_bias,
    output_weight,
    output_bias,
    second_gain,
    second_bias,
    inner_weight,
    inner_bias,
    outer_weight,
    outer_bias,
    block_owner,
    cotangent,
):
    local_rows, model_width = tokens.shape
    heads_here = mixer_weight.shape[2] // HD
    piece_rows = local_rows * lax.axis_size("tp")
    blocks = piece_rows // BLOCK
    unit_count = piece_rows * lax.axis_size("ctx") // SHORT
    owners = block_owner[0]
    block_index = jnp.arange(blocks)
    member = (owners[:, None] == jnp.arange(unit_count)[None, :]).astype(jnp.float32)
    earlier = (
        (owners[:, None] == owners[None, :]) & (block_index[:, None] > block_index[None, :])
    ).astype(jnp.float32)
    causal = jnp.arange(BLOCK)[:, None] >= jnp.arange(BLOCK)[None, :]
    inputs = tokens.astype(jnp.float32)
    first_normed, first_pull = jax.vjp(
        layer_norm, inputs, first_gain.astype(jnp.float32), first_bias.astype(jnp.float32)
    )
    first_low = first_normed.astype(jnp.bfloat16)
    first_rows = lax.all_gather(first_low, "tp", axis=0, tiled=True)
    mixer_flat = mixer_weight.reshape(model_width, -1)
    mixed_rows = jnp.dot(
        first_rows, mixer_flat, preferred_element_type=jnp.float32
    ) + mixer_bias.astype(jnp.float32).reshape(-1)
    mixed_low = mixed_rows.astype(jnp.bfloat16).reshape(piece_rows, 3, heads_here, HD)
    query_rows = mixed_low[:, 0]
    key_rows = mixed_low[:, 1]
    value_rows = mixed_low[:, 2]
    weight_float = feature_weight.astype(jnp.float32)
    bias_float = feature_bias.astype(jnp.float32)
    query_lifted, query_pull = jax.vjp(
        feature_map, query_rows.astype(jnp.float32), weight_float[0], bias_float[0]
    )
    key_lifted, key_pull = jax.vjp(
        feature_map, key_rows.astype(jnp.float32), weight_float[1], bias_float[1]
    )
    query_blocks = query_lifted.astype(jnp.bfloat16).reshape(blocks, BLOCK, heads_here, 2 * HD)
    key_blocks = key_lifted.astype(jnp.bfloat16).reshape(blocks, BLOCK, heads_here, 2 * HD)
    value_blocks = value_rows.reshape(blocks, BLOCK, heads_here, HD)
    block_state = jnp.einsum(
        "jthe,jthf->jhef", value_blocks, key_blocks, preferred_element_type=jnp.float32
    )
    block_norm = jnp.sum(key_blocks.astype(jnp.float32), axis=1)
    totals = (
        jnp.einsum("js,jhef->shef", member, block_state, precision=HIGHEST),
        jnp.einsum("js,jhf->shf", member, block_norm, precision=HIGHEST),
    )
    incoming = entering(
        (totals[0], totals[1]),
        "ctx",
        add_pair,
        (jnp.zeros_like(totals[0]), jnp.zeros_like(totals[1])),
        False,
    )
    state_before = jnp.einsum(
        "ji,ihef->jhef", earlier, block_state, precision=HIGHEST
    ) + jnp.einsum("js,shef->jhef", member, incoming[0], precision=HIGHEST)
    norm_before = jnp.einsum("ji,ihf->jhf", earlier, block_norm, precision=HIGHEST) + jnp.einsum(
        "js,shf->jhf", member, incoming[1], precision=HIGHEST
    )
    numerator = jnp.einsum(
        "jthf,jhef->jthe",
        query_blocks,
        state_before,
        precision=HIGHEST,
        preferred_element_type=jnp.float32,
    )
    denominator = jnp.einsum(
        "jthf,jhf->jth",
        query_blocks,
        norm_before,
        precision=HIGHEST,
        preferred_element_type=jnp.float32,
    )
    scores = jnp.einsum(
        "jthf,jshf->jhts", query_blocks, key_blocks, preferred_element_type=jnp.float32
    )
    scores_low = jnp.where(causal, scores, 0.0).astype(jnp.bfloat16)
    numerator = numerator + jnp.einsum(
        "jhts,jshe->jthe", scores_low, value_blocks, preferred_element_type=jnp.float32
    )
    denominator = denominator + jnp.swapaxes(jnp.sum(scores_low.astype(jnp.float32), axis=-1), 1, 2)
    attended = numerator / denominator[..., None]
    attended_low = attended.astype(jnp.bfloat16).reshape(piece_rows, heads_here * HD)
    attention_sum = lax.psum_scatter(
        jnp.dot(attended_low, output_weight, preferred_element_type=jnp.float32),
        "tp",
        scatter_dimension=0,
        tiled=True,
    )
    middle = inputs + attention_sum + output_bias.astype(jnp.float32)
    second_normed, second_pull = jax.vjp(
        layer_norm, middle, second_gain.astype(jnp.float32), second_bias.astype(jnp.float32)
    )
    second_low = second_normed.astype(jnp.bfloat16)
    second_rows = lax.all_gather(second_low, "tp", axis=0, tiled=True)
    hidden_input = jnp.dot(
        second_rows, inner_weight, preferred_element_type=jnp.float32
    ) + inner_bias.astype(jnp.float32)
    activated_float, curve_pull = jax.vjp(gaussian_unit, hidden_input)
    activated = activated_float.astype(jnp.bfloat16)
    branch_out = lax.psum_scatter(
        jnp.dot(activated, outer_weight, preferred_element_type=jnp.float32).astype(jnp.bfloat16),
        "tp",
        scatter_dimension=0,
        tiled=True,
    ).astype(jnp.float32)
    result = (middle + branch_out + outer_bias.astype(jnp.float32)).astype(jnp.bfloat16)
    upstream = cotangent.astype(jnp.float32)
    upstream_rows = lax.all_gather(cotangent, "tp", axis=0, tiled=True)
    outer_delta = jnp.einsum(
        "tf,td->fd", activated, upstream_rows, preferred_element_type=jnp.float32
    )
    activated_delta = jnp.einsum(
        "td,fd->tf", upstream_rows, outer_weight, preferred_element_type=jnp.float32
    )
    (hidden_delta,) = curve_pull(activated_delta)
    hidden_low = hidden_delta.astype(jnp.bfloat16)
    inner_bias_delta = jnp.sum(hidden_low.astype(jnp.float32), axis=0)
    inner_delta = jnp.einsum(
        "td,tf->df", second_rows, hidden_low, preferred_element_type=jnp.float32
    )
    second_delta = lax.psum_scatter(
        jnp.einsum("tf,df->td", hidden_low, inner_weight, preferred_element_type=jnp.float32),
        "tp",
        scatter_dimension=0,
        tiled=True,
    )
    middle_back, second_gain_part, second_bias_part = second_pull(second_delta)
    middle_delta = upstream + middle_back
    middle_low = middle_delta.astype(jnp.bfloat16)
    middle_rows = lax.all_gather(middle_low, "tp", axis=0, tiled=True)
    output_delta = jnp.einsum(
        "tk,td->kd", attended_low, middle_rows, preferred_element_type=jnp.float32
    )
    attended_delta = rounded(
        jnp.einsum("td,kd->tk", middle_rows, output_weight, preferred_element_type=jnp.float32)
    )
    attended_delta = attended_delta.reshape(blocks, BLOCK, heads_here, HD)
    numerator_delta = attended_delta / denominator[..., None]
    denominator_delta = -jnp.sum(attended_delta * attended, axis=-1) / denominator
    score_delta = (
        jnp.einsum(
            "jthe,jshe->jhts",
            numerator_delta,
            value_blocks,
            precision=HIGHEST,
            preferred_element_type=jnp.float32,
        )
        + jnp.swapaxes(denominator_delta, 1, 2)[..., None]
    )
    score_low = jnp.where(causal, score_delta, 0.0).astype(jnp.bfloat16)
    value_delta = jnp.einsum(
        "jhts,jthe->jshe",
        scores_low,
        numerator_delta,
        precision=HIGHEST,
        preferred_element_type=jnp.float32,
    )
    query_delta = (
        jnp.einsum("jhts,jshf->jthf", score_low, key_blocks, preferred_element_type=jnp.float32)
        + jnp.einsum(
            "jthe,jhef->jthf",
            numerator_delta,
            state_before,
            precision=HIGHEST,
            preferred_element_type=jnp.float32,
        )
        + denominator_delta[..., None] * norm_before[:, None]
    )
    key_delta = jnp.einsum(
        "jhts,jthf->jshf", score_low, query_blocks, preferred_element_type=jnp.float32
    )
    before_delta = jnp.einsum(
        "jthf,jthe->jhef",
        query_blocks,
        numerator_delta,
        precision=HIGHEST,
        preferred_element_type=jnp.float32,
    )
    norm_before_delta = jnp.einsum(
        "jthf,jth->jhf",
        query_blocks,
        denominator_delta,
        precision=HIGHEST,
        preferred_element_type=jnp.float32,
    )
    leaving = (
        jnp.einsum("js,jhef->shef", member, before_delta, precision=HIGHEST),
        jnp.einsum("js,jhf->shf", member, norm_before_delta, precision=HIGHEST),
    )
    later_sums = entering(
        (leaving[0], leaving[1]),
        "ctx",
        add_pair,
        (jnp.zeros_like(leaving[0]), jnp.zeros_like(leaving[1])),
        True,
    )
    state_delta = jnp.einsum(
        "ji,jhef->ihef", earlier, before_delta, precision=HIGHEST
    ) + jnp.einsum("js,shef->jhef", member, later_sums[0], precision=HIGHEST)
    block_norm_delta = jnp.einsum(
        "ji,jhf->ihf", earlier, norm_before_delta, precision=HIGHEST
    ) + jnp.einsum("js,shf->jhf", member, later_sums[1], precision=HIGHEST)
    value_delta = value_delta + jnp.einsum(
        "jhef,jthf->jthe",
        state_delta,
        key_blocks,
        precision=HIGHEST,
        preferred_element_type=jnp.float32,
    )
    key_delta = (
        key_delta
        + jnp.einsum(
            "jhef,jthe->jthf",
            state_delta,
            value_blocks,
            precision=HIGHEST,
            preferred_element_type=jnp.float32,
        )
        + block_norm_delta[:, None]
    )
    query_in_delta, query_weight_delta, query_bias_delta = query_pull(
        rounded(query_delta).reshape(piece_rows, heads_here, 2 * HD)
    )
    key_in_delta, key_weight_delta, key_bias_delta = key_pull(
        rounded(key_delta).reshape(piece_rows, heads_here, 2 * HD)
    )
    mixed_delta = jnp.stack(
        [query_in_delta, key_in_delta, value_delta.reshape(piece_rows, heads_here, HD)], axis=1
    )
    mixed_delta = mixed_delta.astype(jnp.bfloat16).reshape(piece_rows, 3 * heads_here * HD)
    mixer_bias_delta = jnp.sum(mixed_delta.astype(jnp.float32), axis=0).reshape(3, heads_here * HD)
    mixer_delta = jnp.einsum(
        "td,tk->dk", first_rows, mixed_delta, preferred_element_type=jnp.float32
    ).reshape(model_width, 3, heads_here * HD)
    first_delta = lax.psum_scatter(
        jnp.einsum("tk,dk->td", mixed_delta, mixer_flat, preferred_element_type=jnp.float32).astype(
            jnp.bfloat16
        ),
        "tp",
        scatter_dimension=0,
        tiled=True,
    ).astype(jnp.float32)
    input_back, first_gain_part, first_bias_part = first_pull(first_delta)
    tokens_delta = middle_delta + input_back
    feature_weight_delta = jnp.stack([query_weight_delta, key_weight_delta])
    feature_bias_delta = jnp.stack([query_bias_delta, key_bias_delta])
    output_bias_part = jnp.sum(middle_delta, axis=0)
    outer_bias_part = jnp.sum(upstream, axis=0)
    summed = lax.psum(
        (
            mixer_delta,
            mixer_bias_delta,
            feature_weight_delta,
            feature_bias_delta,
            output_delta,
            inner_delta,
            inner_bias_delta,
            outer_delta,
            first_gain_part,
            first_bias_part,
            output_bias_part,
            second_gain_part,
            second_bias_part,
            outer_bias_part,
        ),
        ("dp", "ctx"),
    )
    shared = lax.psum((summed[8], summed[9], summed[10], summed[11], summed[12], summed[13]), "tp")
    return (
        result,
        tokens_delta,
        shared[0],
        shared[1],
        summed[0],
        summed[1],
        summed[2],
        summed[3],
        summed[4],
        shared[2],
        shared[3],
        shared[4],
        summed[5],
        summed[6],
        summed[7],
        shared[5],
    )


def solution(mesh):
    in_specs = (
        P(("dp", "ctx", "tp"), None),
        P(),
        P(),
        P(None, None, "tp"),
        P(None, "tp"),
        P(None, "tp", None, None),
        P(None, "tp", None),
        P("tp", None),
        P(),
        P(),
        P(),
        P(None, "tp"),
        P("tp"),
        P("tp", None),
        P(),
        P("dp", None),
        P(("dp", "ctx", "tp"), None),
    )
    out_specs = (
        P(("dp", "ctx", "tp"), None),
        P(("dp", "ctx", "tp"), None),
        P(),
        P(),
        P(None, None, "tp"),
        P(None, "tp"),
        P(None, "tp", None, None),
        P(None, "tp", None),
        P("tp", None),
        P(),
        P(),
        P(),
        P(None, "tp"),
        P("tp"),
        P("tp", None),
        P(),
    )
    return jax.shard_map(shards, mesh=mesh, in_specs=in_specs, out_specs=out_specs, check_vma=False)
```

profile of v0, /device:TPU:0, one launch (start us, length us, event | category | flops | bytes accessed | tf_op | source)
XLA Modules:
  0.0 1006.3 jit_solution(10132067115701984201)
XLA Ops:
  14.2 65.0 %all-gather.11.cloned.1.call-done = bf16[2048,768]{1,0:T(8,128)(2,1)} async-done(((bf16[512,768]{1,0:T(8,128)(2,1)}), bf16[2048,768]{1,0:T(8,128)(2,1)}) %all-gather.11.cloned.1.call-update) | async-done | bytes 3145744 | tf_op jit(solution)/shard_map/all_gather | solution.py:95
  121.6 5.6 all-gather.4
  147.0 7.0 all-gather
  154.0 6.5 while.34
  161.7 5.7 multiply_add_fusion.3
  171.9 4.7 fusion.25
  189.6 108.3 %reduce-scatter.5.cloned.1.call-done = f32[512,768]{1,0:T(8,128)} async-done(((f32[2048,768]{1,0:T(8,128)}), f32[512,768]{1,0:T(8,128)}) %reduce-scatter.5.cloned.1.call-update) | async-done | bytes 1572880 | tf_op jit(solution)/shard_map/reduce_scatter | solution.py:160
  303.6 62.3 %all-gather.13.cloned.1.call-done = bf16[2048,768]{1,0:T(8,128)(2,1)} async-done(((bf16[512,768]{1,0:T(8,128)(2,1)}), bf16[2048,768]{1,0:T(8,128)(2,1)}) %all-gather.13.cloned.1.call-update) | async-done | bytes 3145744 | tf_op jit(solution)/shard_map/all_gather | solution.py:171
  365.9 7.5 fusion.128
  373.4 56.1 %all-gather.15.cloned.1.call-done = bf16[2048,768]{1,0:T(8,128)(2,1)} async-done(((bf16[512,768]{1,0:T(8,128)(2,1)}), bf16[2048,768]{1,0:T(8,128)(2,1)}) %all-gather.15.cloned.1.call-update) | async-done | bytes 3145744 | tf_op jit(solution)/shard_map/all_gather | solution.py:185
  429.5 12.2 %convert_reduce_fusion = (f32[768]{0:T(1024)}, bf16[2048,768]{1,0:T(8,128)(2,1)S(1)}, bf16[2048,768]{1,0:T(8,128)(2,1)}) fusion(f32[2048,768]{1,0:T(8,128)} %fusion.128, f32[768]{0:T(1024)} %convert_element_type.136, bf16[2048,768]{1,0:T(8,128)(2,1)} %all-gather.15.cloned.1.call-done, bf16[768,768]{1,0:T(8,128)(2,1)S(1)} %copy-done), kind=kOutput, calls=%fused_computation.18 | convolution fusion | flops 2461531392 | bytes 16914432 | tf_op jit(solution)/shard_map/td,fd->tf/dot_general | solution.py:189
  443.4 4.6 fusion.129
  448.1 6.3 convolution_convert_fusion
  455.0 102.6 %reduce-scatter.9.cloned.1.call-done = f32[512,768]{1,0:T(8,128)} async-done(((f32[2048,768]{1,0:T(8,128)}), f32[512,768]{1,0:T(8,128)}) %reduce-scatter.9.cloned.1.call-update) | async-done | bytes 1572880 | tf_op jit(solution)/shard_map/reduce_scatter | solution.py:198
  560.2 60.3 %reduce-scatter.7.cloned.1.call-done = bf16[512,768]{1,0:T(8,128)(2,1)} async-done(((bf16[2048,768]{1,0:T(8,128)(2,1)}), bf16[512,768]{1,0:T(8,128)(2,1)}) %reduce-scatter.7.cloned.1.call-update) | async-done | bytes 786448 | tf_op jit(solution)/shard_map/reduce_scatter | solution.py:177
  629.5 60.4 %all-gather.17.cloned.1.call-done = bf16[2048,768]{1,0:T(8,128)(2,1)} async-done(((bf16[512,768]{1,0:T(8,128)(2,1)}), bf16[2048,768]{1,0:T(8,128)(2,1)}) %all-gather.17.cloned.1.call-update) | async-done | bytes 3145744 | tf_op jit(solution)/shard_map/all_gather | solution.py:207
  695.6 5.2 multiply_reduce_fusion
  701.0 10.8 %fusion.23 = f32[32,3,128,64]{2,3,1,0:T(8,128)} fusion(f32[32,3,64,128]{3,0,2,1:T(8,128)S(1)} %copy-done.27, f32[32,64,3,64]{1,0,3,2:T(8,128)S(1)} %copy-done.24, f32[32,64,3]{1,2,0:T(4,128)S(1)} %copy-done.56), kind=kOutput, calls=%fused_computation.50 | convolution fusion | flops 604372992 | bytes 7888896 | tf_op jit(solution)/shard_map/jthe,jhef->jthf/dot_general | solution.py:237
  711.8 4.3 fusion.111
  717.6 5.2 all-gather.5
  725.7 6.5 all-gather.2
  733.0 5.7 multiply_add_fusion.2
  738.7 4.8 fusion.15
  743.6 4.5 fusion.17
  748.1 4.4 select_convert_fusion
  756.5 4.9 bitcast_add_fusion
  797.4 4.9 fusion.113
  810.5 7.0 fusion.132
  830.0 39.3 %reduce-scatter.11.cloned.1.call-done = bf16[512,768]{1,0:T(8,128)(2,1)} async-done(((bf16[2048,768]{1,0:T(8,128)(2,1)}), bf16[512,768]{1,0:T(8,128)(2,1)}) %reduce-scatter.11.cloned.1.call-update) | async-done | bytes 786448 | tf_op jit(solution)/shard_map/reduce_scatter | solution.py:312
  875.3 26.5 %all-reduce = (f32[768]{0:T(1024)S(1)}, f32[768]{0:T(1024)S(1)}, f32[3,192]{1,0:T(4,128)}, f32[2,3,64]{2,1,0:T(4,128)S(1)}, f32[768]{0:T(1024)S(1)}, /*index=5*/...) all-reduce(f32[768]{0:T(1024)S(1)} %get-tuple-element.373, ...), channel_id=1, replica_groups=mesh['dp'=2,'ctx'=4,'tp'=4] {'dp','ctx'}, use_global_device_ids=true, to_apply=%region_32.33 | all-reduce | flops 6336 | bytes 50688 | tf_op jit(solution)/shard_map/psum | solution.py:326
  902.4 18.5 %all-reduce.2 = (f32[768]{0:T(1024)}, f32[768]{0:T(1024)}, f32[768]{0:T(1024)}, f32[768]{0:T(1024)}, f32[768]{0:T(1024)}, /*index=5*/f32[768]{0:T(1024)}) all-reduce(f32[768]{0:T(1024)S(1)} %get-tuple-element.404, f32[768]{0:T(1024)S(1)} %get-tuple-element.405, ...), channel_id=1, replica_groups=mesh['dp'=2,'ctx'=4,'tp'=4] {'tp'}, use_global_device_ids=true, to_apply=%region_33.34 | all-reduce | flops 4608 | bytes 36864 | tf_op jit(solution)/shard_map/psum | solution.py:345
  920.9 70.3 %all-reduce.5.cloned.1.call-done = (f32[768,3,192]{0,2,1:T(8,128)}, f32[2,3,64,64]{3,2,1,0:T(8,128)}, f32[192,768]{1,0:T(8,128)}, f32[768,768]{1,0:T(8,128)}, f32[768,768]{1,0:T(8,128)}) async-done(((f32[768,3,192]{0,2,1:T(8,128)}, f32[2,3,64,64]{3,2,1,0:T(8,128)}, f32[192,768]{1,0:T(8,128)}, f32[768,768]{1,0:T(8,128)}, f32[768,768]{1,0:T(8,128)}), (f32[768,3,192]{0,2,1:T(8,128)}, ...) | async-done | bytes 7176208 | tf_op jit(solution)/shard_map/psum | solution.py:326
  (369 shorter events, 199.6 us)
Async XLA Ops:
  7.2 422.3 %copy-start = (bf16[768,768]{1,0:T(8,128)(2,1)S(1)}, bf16[768,768]{1,0:T(8,128)(2,1)}, u32[]{:S(2)}) copy-start(bf16[768,768]{1,0:T(8,128)(2,1)} %param.34) | copy-start | bytes 3538948
  7.2 72.0 %all-gather.11.cloned.1.call-start = ((), (), s32[]{:S(2)}) async-start(), calls=%async_computation.4 | async-start | bytes 3932160 | tf_op jit(solution)/shard_map/all_gather | solution.py:95
  8.8 70.4 %copy-start.98 = (bf16[768,3,192]{0,2,1:T(8,128)(2,1)S(1)}, bf16[768,3,192]{0,2,1:T(8,128)(2,1)}, u32[]{:S(2)}) copy-start(bf16[768,3,192]{0,2,1:T(8,128)(2,1)} %param.24) | copy-start | bytes 2654212
  12.8 285.1 %reduce-scatter.5.cloned.1.call-start = ((), (), s32[]{:S(2)}) async-start(), calls=%async_computation.5 | async-start | bytes 7864320 | tf_op jit(solution)/shard_map/reduce_scatter | solution.py:160
  87.5 22.8 %copy-start.5 = (f32[2048,3,64]{0,2,1:T(8,128)}, f32[2048,3,64]{0,2,1:T(8,128)S(1)}, u32[]{:S(2)}) copy-start(f32[2048,3,64]{0,2,1:T(8,128)S(1)} %get-tuple-element.454) | copy-start | bytes 4718596
  117.1 10.1 %copy-start.11 = (f32[2048,3,64]{0,2,1:T(8,128)S(1)}, f32[2048,3,64]{0,2,1:T(8,128)}, u32[]{:S(2)}) copy-start(f32[2048,3,64]{0,2,1:T(8,128)} %get-tuple-element.448) | copy-start | bytes 4718596
  117.1 10.1 %copy-start.48 = (f32[2048,3]{0,1:T(4,128)S(1)}, f32[2048,3]{0,1:T(4,128)}, u32[]{:S(2)}) copy-start(f32[2048,3]{0,1:T(4,128)} %get-tuple-element.447) | copy-start | bytes 73732
  161.7 7.7 copy-start.71
  169.3 7.3 copy-start.57
  169.4 7.3 copy-start.100
  188.3 177.6 %all-gather.13.cloned.1.call-start = ((), (), s32[]{:S(2)}) async-start(), calls=%async_computation.6 | async-start | bytes 3932160 | tf_op jit(solution)/shard_map/all_gather | solution.py:171
  301.7 127.8 %all-gather.15.cloned.1.call-start = ((), (), s32[]{:S(2)}) async-start(), calls=%async_computation.8 | async-start | bytes 3932160 | tf_op jit(solution)/shard_map/all_gather | solution.py:185
  302.3 255.3 %reduce-scatter.9.cloned.1.call-start = ((), (), s32[]{:S(2)}) async-start(), calls=%async_computation.9 | async-start | bytes 7864320 | tf_op jit(solution)/shard_map/reduce_scatter | solution.py:198
  429.5 13.9 %copy-start.97 = (bf16[768,768]{1,0:T(8,128)(2,1)S(1)}, bf16[768,768]{1,0:T(8,128)(2,1)}, u32[]{:S(2)}) copy-start(bf16[768,768]{1,0:T(8,128)(2,1)} %param.32) | copy-start | bytes 3538948
  448.0 172.5 %reduce-scatter.7.cloned.1.call-start = ((), (), s32[]{:S(2)}) async-start(), calls=%async_computation.7 | async-start | bytes 3932160 | tf_op jit(solution)/shard_map/reduce_scatter | solution.py:177
  454.4 235.5 %all-gather.17.cloned.1.call-start = ((), (), s32[]{:S(2)}) async-start(), calls=%async_computation.10 | async-start | bytes 3932160 | tf_op jit(solution)/shard_map/all_gather | solution.py:207
  455.0 105.2 %copy-start.79 = (f32[512]{0:T(512)S(1)}, f32[512]{0:T(512)}, u32[]{:S(2)}) copy-start(f32[512]{0:T(512)} %copy-done.78) | copy-start | bytes 6148
  560.2 64.8 %copy-start.32 = (bf16[512,768]{1,0:T(8,128)(2,1)S(1)}, bf16[512,768]{1,0:T(8,128)(2,1)}, u32[]{:S(2)}) copy-start(bf16[512,768]{1,0:T(8,128)(2,1)} %param.37) | copy-start | bytes 2359300
  625.0 64.9 %copy-start.53 = (bf16[192,768]{1,0:T(8,128)(2,1)S(1)}, bf16[192,768]{1,0:T(8,128)(2,1)}, u32[]{:S(2)}) copy-start(bf16[192,768]{1,0:T(8,128)(2,1)} %param.28) | copy-start | bytes 884740
  626.2 243.1 %reduce-scatter.11.cloned.1.call-start = ((), (), s32[]{:S(2)}) async-start(), calls=%async_computation.11 | async-start | bytes 3932160 | tf_op jit(solution)/shard_map/reduce_scatter | solution.py:312
  692.9 7.9 copy-start.58
  693.0 7.9 copy-start.62
  701.0 10.8 %copy-start.23 = (bf16[32,64,3,128]{3,1,2,0:T(8,128)(2,1)S(1)}, bf16[32,64,3,128]{3,1,2,0:T(8,128)(2,1)}, u32[]{:S(2)}) copy-start(bf16[32,64,3,128]{3,1,2,0:T(8,128)(2,1)} %copy-done.22) | copy-start | bytes 4718596
  716.1 9.5 copy-start.28
  725.7 7.3 copy-start.87
  810.2 181.0 %all-reduce.5.cloned.1.call-start = ((), (), s32[]{:S(2)}) async-start(), calls=%async_computation.12 | async-start | bytes 14548992 | tf_op jit(solution)/shard_map/psum | solution.py:326
  817.5 7.2 copy-start.38
  829.8 39.5 %copy-start.68 = (f32[768]{0:T(1024)S(1)}, f32[768]{0:T(1024)}, u32[]{:S(2)}) copy-start(f32[768]{0:T(1024)} %copy-done.67) | copy-start | bytes 9220
  829.8 39.5 %copy-start.70 = (f32[512]{0:T(512)S(1)}, f32[512]{0:T(512)}, u32[]{:S(2)}) copy-start(f32[512]{0:T(512)} %copy-done.69) | copy-start | bytes 6148
  829.9 41.3 %copy-start.77 = (f32[512]{0:T(512)S(1)}, f32[512]{0:T(512)}, u32[]{:S(2)}) copy-start(f32[512]{0:T(512)} %copy-done.76) | copy-start | bytes 6148
  829.9 41.3 %copy-start.74 = (f32[512]{0:T(512)S(1)}, f32[512]{0:T(512)}, u32[]{:S(2)}) copy-start(f32[512]{0:T(512)} %copy-done.73) | copy-start | bytes 6148
  830.0 43.3 %copy-start.19 = (f32[512,768]{1,0:T(8,128)S(1)}, f32[512,768]{1,0:T(8,128)}, u32[]{:S(2)}) copy-start(f32[512,768]{1,0:T(8,128)} %copy-done.18) | copy-start | bytes 4718596
  (81 other events, 260.8 us)
Sparse Core Ops, SparseCore 0:
  12.9 66.1 all-gather.10
  188.4 109.4 reduce-scatter.4
  301.8 64.0 all-gather.12
  367.3 62.1 all-gather.14
  448.2 109.3 reduce-scatter.8
  559.8 60.7 reduce-scatter.6
  626.3 63.5 all-gather.16
  810.4 58.9 reduce-scatter.10
  874.4 116.7 all-reduce.4
where the time goes:
time: 1020 us; the launch traced here: 1010 us
  waiting for transfers between devices  625 us (61%)
  matrix products  136 us (13%)
  local copies, waits for them, and re-layouts  86.1 us (8%)
  other arithmetic  72.6 us (7%)
  blocking collectives  69.3 us (7%)
  between operations  15.4 us (2%)
    reduce_scatter x1, waiting for transfers between devices, shards(): lax.psum_scatter(jnp.dot(attended_low, output_weight, preferred_element_t...  108 us
    reduce_scatter x1, waiting for transfers between devices, shards(): lax.psum_scatter(jnp.einsum('tf,df->td', hidden_low, inner_weight, prefer...  103 us
    psum x1, waiting for transfers between devices, shards(): lax.psum((mixer_delta, mixer_bias_delta, feature_weight_delta, feature_bi...  70.3 us
    all_gather x1, waiting for transfers between devices, shards(): first_rows = lax.all_gather(first_low, 'tp', axis=0, tiled=True)  65 us
    all_gather x1, waiting for transfers between devices, shards(): second_rows = lax.all_gather(second_low, 'tp', axis=0, tiled=True)  62.3 us
    all_gather x1, waiting for transfers between devices, shards(): middle_rows = lax.all_gather(middle_low, 'tp', axis=0, tiled=True)  60.4 us
    reduce_scatter x1, waiting for transfers between devices, shards(): lax.psum_scatter(jnp.dot(activated, outer_weight, preferred_element_type=...  60.3 us
    all_gather x1, waiting for transfers between devices, shards(): upstream_rows = lax.all_gather(cotangent, 'tp', axis=0, tiled=True)  56.1 us
  transfers between devices with their start and end apart: 9, of which 9 were waited for; matrix products, arithmetic and copies ran while one was open for 5% of the time, Pallas kernels for 0%

commit v1 on v0

--- a/solution.py
+++ b/solution.py
@@ -168,7 +168,8 @@
         layer_norm, middle, second_gain.astype(jnp.float32), second_bias.astype(jnp.float32)
     )
     second_low = second_normed.astype(jnp.bfloat16)
-    second_rows = lax.all_gather(second_low, "tp", axis=0, tiled=True)
+    sent = jnp.stack([second_low] * lax.axis_size("tp"))
+    second_rows = jnp.concatenate(lax.all_to_all(sent, "tp", 0, 0), axis=0)
     hidden_input = jnp.dot(
         second_rows, inner_weight, preferred_element_type=jnp.float32
     ) + inner_bias.astype(jnp.float32)

time: 1020 us -> 1020 us (level)
    all_to_all x0 -> x1, waiting for transfers between devices: none -> 120 us  [shards(): second_rows = jnp.concatenate(lax.all_to_all(sent, 'tp', 0, 0), axis=0)]
    all_gather x1 -> x0, waiting for transfers between devices: 62.3 us -> none  [shards(): second_rows = lax.all_gather(second_low, 'tp', axis=0, tiled=True)]
    all_gather x1, waiting for transfers between devices: 56.1 us -> 0.01 us  [shards(): upstream_rows = lax.all_gather(cotangent, 'tp', axis=0, tiled=True)]
  transfers between devices with their start and end apart: 9 -> 9, of which waited for: 9 -> 8; matrix products, arithmetic and copies ran while one was open for 5% -> 5% of each run, Pallas kernels for 0% -> 0%
where the time goes in v1:
time: 1020 us; the launch traced here: 1010 us
  waiting for transfers between devices  626 us (61%)
  matrix products  136 us (13%)
  local copies, waits for them, and re-layouts  87.9 us (9%)
  other arithmetic  71.7 us (7%)
  blocking collectives  69.3 us (7%)
  between operations  15.7 us (2%)
    all_to_all x1, waiting for transfers between devices, shards(): second_rows = jnp.concatenate(lax.all_to_all(sent, 'tp', 0, 0), axis=0)  120 us
    reduce_scatter x1, waiting for transfers between devices, shards(): lax.psum_scatter(jnp.dot(attended_low, output_weight, preferred_element_t...  108 us
    reduce_scatter x1, waiting for transfers between devices, shards(): lax.psum_scatter(jnp.einsum('tf,df->td', hidden_low, inner_weight, prefer...  102 us
    psum x1, waiting for transfers between devices, shards(): lax.psum((mixer_delta, mixer_bias_delta, feature_weight_delta, feature_bi...  70.3 us
    all_gather x1, waiting for transfers between devices, shards(): first_rows = lax.all_gather(first_low, 'tp', axis=0, tiled=True)  65 us
    all_gather x1, waiting for transfers between devices, shards(): middle_rows = lax.all_gather(middle_low, 'tp', axis=0, tiled=True)  60.5 us
    reduce_scatter x1, waiting for transfers between devices, shards(): lax.psum_scatter(jnp.dot(activated, outer_weight, preferred_element_type=...  60.3 us
    reduce_scatter x1, waiting for transfers between devices, shards(): lax.psum_scatter(jnp.einsum('tk,dk->td', mixed_delta, mixer_flat, preferr...  39.3 us
  transfers between devices with their start and end apart: 9, of which 8 were waited for; matrix products, arithmetic and copies ran while one was open for 5% of the time, Pallas kernels for 0%

profile of v1, /device:TPU:0, one launch (start us, length us, event | category | flops | bytes accessed | tf_op | source)
XLA Modules:
  0.0 1013.2 jit_solution(3089321646345442224)
XLA Ops:
  14.2 65.0 %all-gather.10.cloned.1.call-done = bf16[2048,768]{1,0:T(8,128)(2,1)} async-done(((bf16[512,768]{1,0:T(8,128)(2,1)}), bf16[2048,768]{1,0:T(8,128)(2,1)}) %all-gather.10.cloned.1.call-update) | async-done | bytes 3145744 | tf_op jit(solution)/shard_map/all_gather | solution.py:95
  121.5 5.6 all-gather.4
  147.0 7.0 all-gather
  154.0 6.5 while.34
  161.7 5.7 multiply_add_fusion.3
  171.9 4.7 fusion.25
  189.5 108.3 %reduce-scatter.5.cloned.1.call-done = f32[512,768]{1,0:T(8,128)} async-done(((f32[2048,768]{1,0:T(8,128)}), f32[512,768]{1,0:T(8,128)}) %reduce-scatter.5.cloned.1.call-update) | async-done | bytes 1572880 | tf_op jit(solution)/shard_map/reduce_scatter | solution.py:160
  302.6 4.7 all-to-all-start
  309.4 119.8 %all-to-all-done = bf16[4,512,768]{2,1,0:T(8,128)(2,1)} async-done(((bf16[4,512,768]{2,1,0:T(8,128)(2,1)}), bf16[4,512,768]{2,1,0:T(8,128)(2,1)}, u32[]{:S(2)}, u32[]{:S(2)}) %all-to-all-start) | async-done | bytes 3145760 | tf_op jit(solution)/shard_map/all_to_all | solution.py:172
  429.2 7.5 fusion.128
  436.7 12.2 %convert_reduce_fusion = (f32[768]{0:T(1024)}, bf16[2048,768]{1,0:T(8,128)(2,1)S(1)}, bf16[2048,768]{1,0:T(8,128)(2,1)}) fusion(f32[2048,768]{1,0:T(8,128)} %fusion.128, f32[768]{0:T(1024)} %convert_element_type.136, bf16[2048,768]{1,0:T(8,128)(2,1)} %all-gather.12.cloned.1.call-done, bf16[768,768]{1,0:T(8,128)(2,1)S(1)} %copy-done), kind=kOutput, calls=%fused_computation.18 | convolution fusion | flops 2461531392 | bytes 16914432 | tf_op jit(solution)/shard_map/td,fd->tf/dot_general | solution.py:190
  450.6 4.6 fusion.129
  455.3 6.2 convolution_convert_fusion
  462.1 102.1 %reduce-scatter.9.cloned.1.call-done = f32[512,768]{1,0:T(8,128)} async-done(((f32[2048,768]{1,0:T(8,128)}), f32[512,768]{1,0:T(8,128)}) %reduce-scatter.9.cloned.1.call-update) | async-done | bytes 1572880 | tf_op jit(solution)/shard_map/reduce_scatter | solution.py:199
  566.9 60.3 %reduce-scatter.7.cloned.1.call-done = bf16[512,768]{1,0:T(8,128)(2,1)} async-done(((bf16[2048,768]{1,0:T(8,128)(2,1)}), bf16[512,768]{1,0:T(8,128)(2,1)}) %reduce-scatter.7.cloned.1.call-update) | async-done | bytes 786448 | tf_op jit(solution)/shard_map/reduce_scatter | solution.py:178
  636.1 60.5 %all-gather.14.cloned.1.call-done = bf16[2048,768]{1,0:T(8,128)(2,1)} async-done(((bf16[512,768]{1,0:T(8,128)(2,1)}), bf16[2048,768]{1,0:T(8,128)(2,1)}) %all-gather.14.cloned.1.call-update) | async-done | bytes 3145744 | tf_op jit(solution)/shard_map/all_gather | solution.py:208
  702.2 5.2 multiply_reduce_fusion
  707.6 10.8 %fusion.23 = f32[32,3,128,64]{2,3,1,0:T(8,128)} fusion(f32[32,3,64,128]{3,0,2,1:T(8,128)S(1)} %copy-done.27, f32[32,64,3,64]{1,0,3,2:T(8,128)S(1)} %copy-done.24, f32[32,64,3]{1,2,0:T(4,128)S(1)} %copy-done.56), kind=kOutput, calls=%fused_computation.50 | convolution fusion | flops 604372992 | bytes 7888896 | tf_op jit(solution)/shard_map/jthe,jhef->jthf/dot_general | solution.py:238
  718.4 4.3 fusion.111
  724.2 5.2 all-gather.5
  732.3 6.5 all-gather.2
  739.6 5.7 multiply_add_fusion.2
  745.3 4.8 fusion.15
  750.2 4.5 fusion.17
  754.7 4.4 select_convert_fusion
  763.1 4.9 bitcast_add_fusion
  804.0 4.9 fusion.113
  817.0 7.0 fusion.131
  836.5 39.3 %reduce-scatter.11.cloned.1.call-done = bf16[512,768]{1,0:T(8,128)(2,1)} async-done(((bf16[2048,768]{1,0:T(8,128)(2,1)}), bf16[512,768]{1,0:T(8,128)(2,1)}) %reduce-scatter.11.cloned.1.call-update) | async-done | bytes 786448 | tf_op jit(solution)/shard_map/reduce_scatter | solution.py:313
  881.9 26.5 %all-reduce = (f32[768]{0:T(1024)S(1)}, f32[768]{0:T(1024)S(1)}, f32[3,192]{1,0:T(4,128)}, f32[2,3,64]{2,1,0:T(4,128)S(1)}, f32[768]{0:T(1024)S(1)}, /*index=5*/...) all-reduce(f32[768]{0:T(1024)S(1)} %get-tuple-element.373, ...), channel_id=1, replica_groups=mesh['dp'=2,'ctx'=4,'tp'=4] {'dp','ctx'}, use_global_device_ids=true, to_apply=%region_32.33 | all-reduce | flops 6336 | bytes 50688 | tf_op jit(solution)/shard_map/psum | solution.py:327
  909.0 18.5 %all-reduce.2 = (f32[768]{0:T(1024)}, f32[768]{0:T(1024)}, f32[768]{0:T(1024)}, f32[768]{0:T(1024)}, f32[768]{0:T(1024)}, /*index=5*/f32[768]{0:T(1024)}) all-reduce(f32[768]{0:T(1024)S(1)} %get-tuple-element.404, f32[768]{0:T(1024)S(1)} %get-tuple-element.405, ...), channel_id=1, replica_groups=mesh['dp'=2,'ctx'=4,'tp'=4] {'tp'}, use_global_device_ids=true, to_apply=%region_33.34 | all-reduce | flops 4608 | bytes 36864 | tf_op jit(solution)/shard_map/psum | solution.py:346
  927.5 70.3 %all-reduce.5.cloned.1.call-done = (f32[768,3,192]{0,2,1:T(8,128)}, f32[2,3,64,64]{3,2,1,0:T(8,128)}, f32[192,768]{1,0:T(8,128)}, f32[768,768]{1,0:T(8,128)}, f32[768,768]{1,0:T(8,128)}) async-done(((f32[768,3,192]{0,2,1:T(8,128)}, f32[2,3,64,64]{3,2,1,0:T(8,128)}, f32[192,768]{1,0:T(8,128)}, f32[768,768]{1,0:T(8,128)}, f32[768,768]{1,0:T(8,128)}), (f32[768,3,192]{0,2,1:T(8,128)}, ...) | async-done | bytes 7176208 | tf_op jit(solution)/shard_map/psum | solution.py:327
  (369 shorter events, 200.5 us)
Async XLA Ops:
  7.2 429.5 %copy-start = (bf16[768,768]{1,0:T(8,128)(2,1)S(1)}, bf16[768,768]{1,0:T(8,128)(2,1)}, u32[]{:S(2)}) copy-start(bf16[768,768]{1,0:T(8,128)(2,1)} %param.34) | copy-start | bytes 3538948
  7.2 72.0 %all-gather.10.cloned.1.call-start = ((), (), s32[]{:S(2)}) async-start(), calls=%async_computation.5 | async-start | bytes 3932160 | tf_op jit(solution)/shard_map/all_gather | solution.py:95
  8.8 70.4 %copy-start.98 = (bf16[768,3,192]{0,2,1:T(8,128)(2,1)S(1)}, bf16[768,3,192]{0,2,1:T(8,128)(2,1)}, u32[]{:S(2)}) copy-start(bf16[768,3,192]{0,2,1:T(8,128)(2,1)} %param.24) | copy-start | bytes 2654212
  12.8 285.0 %reduce-scatter.5.cloned.1.call-start = ((), (), s32[]{:S(2)}) async-start(), calls=%async_computation.6 | async-start | bytes 7864320 | tf_op jit(solution)/shard_map/reduce_scatter | solution.py:160
  87.4 22.8 %copy-start.5 = (f32[2048,3,64]{0,2,1:T(8,128)}, f32[2048,3,64]{0,2,1:T(8,128)S(1)}, u32[]{:S(2)}) copy-start(f32[2048,3,64]{0,2,1:T(8,128)S(1)} %get-tuple-element.454) | copy-start | bytes 4718596
  117.1 10.1 copy-start.11
  117.1 10.1 copy-start.48
  161.6 7.7 copy-start.71
  169.3 7.3 copy-start.57
  169.3 7.3 copy-start.100
  302.6 126.6 %all-to-all-start = ((bf16[4,512,768]{2,1,0:T(8,128)(2,1)}), bf16[4,512,768]{2,1,0:T(8,128)(2,1)}, u32[]{:S(2)}, u32[]{:S(2)}) async-start(bf16[4,512,768]{2,1,0:T(8,128)(2,1)} %stack.30), calls=%async_computation.1 | async-start | bytes 6291456 | tf_op jit(solution)/shard_map/all_to_all | solution.py:172
  307.3 129.4 %all-gather.12.cloned.1.call-start = ((), (), s32[]{:S(2)}) async-start(), calls=%async_computation.8 | async-start | bytes 3932160 | tf_op jit(solution)/shard_map/all_gather | solution.py:186
  308.0 256.2 %reduce-scatter.9.cloned.1.call-start = ((), (), s32[]{:S(2)}) async-start(), calls=%async_computation.9 | async-start | bytes 7864320 | tf_op jit(solution)/shard_map/reduce_scatter | solution.py:199
  436.7 14.0 %copy-start.97 = (bf16[768,768]{1,0:T(8,128)(2,1)S(1)}, bf16[768,768]{1,0:T(8,128)(2,1)}, u32[]{:S(2)}) copy-start(bf16[768,768]{1,0:T(8,128)(2,1)} %param.32) | copy-start | bytes 3538948
  455.2 172.0 %reduce-scatter.7.cloned.1.call-start = ((), (), s32[]{:S(2)}) async-start(), calls=%async_computation.7 | async-start | bytes 3932160 | tf_op jit(solution)/shard_map/reduce_scatter | solution.py:178
  461.5 235.1 %all-gather.14.cloned.1.call-start = ((), (), s32[]{:S(2)}) async-start(), calls=%async_computation.10 | async-start | bytes 3932160 | tf_op jit(solution)/shard_map/all_gather | solution.py:208
  462.1 104.7 %copy-start.79 = (f32[512]{0:T(512)S(1)}, f32[512]{0:T(512)}, u32[]{:S(2)}) copy-start(f32[512]{0:T(512)} %copy-done.78) | copy-start | bytes 6148
  566.9 64.7 %copy-start.32 = (bf16[512,768]{1,0:T(8,128)(2,1)S(1)}, bf16[512,768]{1,0:T(8,128)(2,1)}, u32[]{:S(2)}) copy-start(bf16[512,768]{1,0:T(8,128)(2,1)} %param.37) | copy-start | bytes 2359300
  631.6 64.9 %copy-start.53 = (bf16[192,768]{1,0:T(8,128)(2,1)S(1)}, bf16[192,768]{1,0:T(8,128)(2,1)}, u32[]{:S(2)}) copy-start(bf16[192,768]{1,0:T(8,128)(2,1)} %param.28) | copy-start | bytes 884740
  632.8 243.1 %reduce-scatter.11.cloned.1.call-start = ((), (), s32[]{:S(2)}) async-start(), calls=%async_computation.11 | async-start | bytes 3932160 | tf_op jit(solution)/shard_map/reduce_scatter | solution.py:313
  699.6 7.9 copy-start.58
  699.6 7.9 copy-start.62
  707.6 10.8 %copy-start.23 = (bf16[32,64,3,128]{3,1,2,0:T(8,128)(2,1)S(1)}, bf16[32,64,3,128]{3,1,2,0:T(8,128)(2,1)}, u32[]{:S(2)}) copy-start(bf16[32,64,3,128]{3,1,2,0:T(8,128)(2,1)} %copy-done.22) | copy-start | bytes 4718596
  722.8 9.5 copy-start.28
  732.3 7.3 copy-start.87
  816.8 181.0 %all-reduce.5.cloned.1.call-start = ((), (), s32[]{:S(2)}) async-start(), calls=%async_computation.12 | async-start | bytes 14548992 | tf_op jit(solution)/shard_map/psum | solution.py:327
  824.1 7.2 copy-start.38
  836.4 39.5 %copy-start.68 = (f32[768]{0:T(1024)S(1)}, f32[768]{0:T(1024)}, u32[]{:S(2)}) copy-start(f32[768]{0:T(1024)} %copy-done.67) | copy-start | bytes 9220
  836.4 39.5 %copy-start.70 = (f32[512]{0:T(512)S(1)}, f32[512]{0:T(512)}, u32[]{:S(2)}) copy-start(f32[512]{0:T(512)} %copy-done.69) | copy-start | bytes 6148
  836.4 41.3 %copy-start.77 = (f32[512]{0:T(512)S(1)}, f32[512]{0:T(512)}, u32[]{:S(2)}) copy-start(f32[512]{0:T(512)} %copy-done.76) | copy-start | bytes 6148
  836.4 41.3 %copy-start.74 = (f32[512]{0:T(512)S(1)}, f32[512]{0:T(512)}, u32[]{:S(2)}) copy-start(f32[512]{0:T(512)} %copy-done.73) | copy-start | bytes 6148
  836.5 43.3 %copy-start.19 = (f32[512,768]{1,0:T(8,128)S(1)}, f32[512,768]{1,0:T(8,128)}, u32[]{:S(2)}) copy-start(f32[512,768]{1,0:T(8,128)} %copy-done.18) | copy-start | bytes 4718596
  (81 other events, 260.5 us)
Sparse Core Ops, SparseCore 0:
  12.9 66.1 all-gather.9
  188.4 109.4 reduce-scatter.4
  309.7 111.9 all-gather.11
  455.3 108.8 reduce-scatter.8
  566.4 60.7 reduce-scatter.6
  632.9 63.5 all-gather.13
  816.9 58.9 reduce-scatter.10
  880.9 116.7 all-reduce.4
